TPU v7x, 32 devices: a whole 2x2x4 slice. The times are simulated.
32 devices in a mesh: row: 16 (over z, x, core), col: 2 (over y).
Axes of the slice: x: 2, y: 2, z: 4, core: 2. Of those that a mesh axis runs over, the one named last changes fastest.
Arguments:
- teacher_hidden: bfloat16 [512, 4608], P('row', 'col'), as said below
- student_hidden: bfloat16 [512, 3584], P('row', 'col'), as said below
- teacher_embed: bfloat16 [16384, 4608], P(('row', 'col')), may hold values from -0.4861359 to 0.4861359
- student_embed: bfloat16 [16384, 3584], P(('row', 'col')), may hold values from -0.5512263 to 0.5512263
Outputs:
- divergence: float32 [512], P(('row', 'col'))
- mean_divergence: float32 [], replicated
Inputs may be any that keep to these rules, and one draw needn't show every extreme that they name: `teacher_hidden`: entries of order one; a few rows may be far larger. `student_hidden`: entries of order one; a few rows may be far larger.
All inputs are finite; a program needn't handle non-finite values.
Results may differ from a plain program's by a relative error of at most 0.0003.
Values may be sent and summed in bfloat16 or wider, within the bound.
A program may use at most 64 MiB of HBM per device.

v0:
```python
import jax
import jax.numpy as jnp
from jax import lax
from jax.sharding import PartitionSpec as P


def block_stats(logit_teacher, logit_student):
    top_teacher = jnp.max(logit_teacher, 1)
    top_student = jnp.max(logit_student, 1)
    weights = jnp.exp(logit_teacher - top_teacher[:, None])
    sum_teacher = jnp.sum(weights, 1)
    cross_term = jnp.sum(weights * (logit_teacher - logit_student), 1)
    sum_student = jnp.sum(jnp.exp(logit_student - top_student[:, None]), 1)
    return (top_teacher, sum_teacher, cross_term, top_student, sum_student)


def per_device(teacher_hidden, student_hidden, teacher_embed, student_embed):
    tokens = teacher_hidden.shape[0] * lax.axis_size("row")
    full_teacher, full_student = (
        lax.all_gather(teacher_hidden, "col", axis=1, tiled=True),
        lax.all_gather(student_hidden, "col", axis=1, tiled=True),
    )
    logit_teacher = jnp.einsum(
        "td,vd->tv",
        lax.all_gather(full_teacher, "row", axis=0, tiled=True),
        teacher_embed,
        preferred_element_type=jnp.float32,
    )
    logit_student = jnp.einsum(
        "td,vd->tv",
        lax.all_gather(full_student, "row", axis=0, tiled=True),
        student_embed,
        preferred_element_type=jnp.float32,
    )
    current = block_stats(logit_teacher, logit_student)
    partial_stats = tuple((fresh_rows for fresh_rows in current))
    top_teacher, sum_teacher, cross_term, top_student, sum_student = partial_stats
    high_teacher, high_student = lax.pmax((top_teacher, top_student), ("row", "col"))
    teacher_scale = jnp.exp(top_teacher - high_teacher)
    student_scale = jnp.exp(top_student - high_student)
    sum_teacher, cross_term, sum_student = lax.psum(
        (sum_teacher * teacher_scale, cross_term * teacher_scale, sum_student * student_scale),
        ("row", "col"),
    )
    top_teacher, top_student = (high_teacher, high_student)
    divergence = (
        cross_term / sum_teacher
        - top_teacher
        - jnp.log(sum_teacher)
        + top_student
        + jnp.log(sum_student)
    )
    mean_divergence = jnp.mean(divergence)
    own_count = tokens // (lax.axis_size("row") * lax.axis_size("col"))
    own_block = lax.axis_index("row") * lax.axis_size("col") + lax.axis_index("col")
    return (lax.dynamic_slice_in_dim(divergence, own_block * own_count, own_count), mean_divergence)


def solution(mesh):
    return jax.shard_map(
        per_device,
        mesh=mesh,
        in_specs=(
            P("row", "col"),
            P("row", "col"),
            P(("row", "col"), None),
            P(("row", "col"), None),
        ),
        out_specs=(P(("row", "col")), P()),
        check_vma=False,
    )
```

profile of v0, /device:TPU:0, one launch (start us, length us, event | category | flops | bytes accessed | tf_op | source)
XLA Modules:
  0.0 213.5 jit_solution(12317152551401748478)
XLA Ops:
  7.2 0.0 all-gather.5.cloned.1.call-start
  7.2 8.6 %all_gather.14 = bf16[32,3584]{1,0:T(8,128)(2,1)} all-gather(bf16[32,1792]{1,0:T(8,128)(2,1)} %param.5), channel_id=1, replica_groups=mesh['row'=16,'col'=2] {'col'}, dimensions={1}, use_global_device_ids=true | all-gather | bytes 344064 | tf_op jit(solution)/shard_map/all_gather | solution.py:21
  15.9 0.0 all-gather.5.cloned.1.call-update
  15.9 0.0 all-gather.3.cloned.1.call-start
  15.9 6.1 %all_gather.12 = bf16[32,4608]{1,0:T(8,128)(2,1)} all-gather(bf16[32,2304]{1,0:T(8,128)(2,1)} %param.4), channel_id=1, replica_groups=mesh['row'=16,'col'=2] {'col'}, dimensions={1}, use_global_device_ids=true | all-gather | bytes 442368 | tf_op jit(solution)/shard_map/all_gather | solution.py:20
  22.1 0.0 all-gather.3.cloned.1.call-update
  22.1 41.9 %all-gather.5.cloned.1.call-done = bf16[512,3584]{1,0:T(8,128)(2,1)} async-done(((bf16[32,3584]{1,0:T(8,128)(2,1)}), bf16[512,3584]{1,0:T(8,128)(2,1)}) %all-gather.5.cloned.1.call-update) | async-done | bytes 3670032 | tf_op jit(solution)/shard_map/all_gather | solution.py:31
  64.0 5.3 %fusion.5 = (f32[512]{0:T(512)S(1)}, f32[512,512]{0,1:T(8,128)S(1)}) fusion(bf16[512,3584]{1,0:T(8,128)(2,1)} %all-gather.5.cloned.1.call-done, bf16[512,3584]{1,0:T(8,128)(2,1)} %param.7), kind=kOutput, calls=%fused_computation.11 | convolution fusion | flops 1879309824 | bytes 8390656 | tf_op jit(solution)/shard_map/td,vd->tv/dot_general | solution.py:29
  69.2 48.9 %all-gather.3.cloned.1.call-done = bf16[512,4608]{1,0:T(8,128)(2,1)} async-done(((bf16[32,4608]{1,0:T(8,128)(2,1)}), bf16[512,4608]{1,0:T(8,128)(2,1)}) %all-gather.3.cloned.1.call-update) | async-done | bytes 4718608 | tf_op jit(solution)/shard_map/all_gather | solution.py:25
  118.1 5.9 %fusion.4 = (f32[512]{0:T(512)S(1)}, f32[512,512]{0,1:T(8,128)S(1)}) fusion(bf16[512,4608]{1,0:T(8,128)(2,1)} %all-gather.3.cloned.1.call-done, bf16[512,4608]{1,0:T(8,128)(2,1)} %param.6), kind=kOutput, calls=%fused_computation.10 | convolution fusion | flops 2416180736 | bytes 10487808 | tf_op jit(solution)/shard_map/td,vd->tv/dot_general | solution.py:23
  124.0 39.2 %all-reduce.1 = (f32[512]{0:T(512)S(1)}, f32[512]{0:T(512)S(1)}) all-reduce(f32[512]{0:T(512)S(1)} %get-tuple-element.16, f32[512]{0:T(512)S(1)} %get-tuple-element.14), channel_id=1, replica_groups=mesh['row'=16,'col'=2] {'row','col'}, use_global_device_ids=true, to_apply=%region_7.0 | all-reduce | flops 1024 | bytes 8192 | tf_op jit(solution)/shard_map/pmax | solution.py:38
  163.3 0.4 multiply_reduce_fusion
  163.7 40.0 %all-reduce = (f32[512]{0:T(512)S(1)}, f32[512]{0:T(512)S(1)}, f32[512]{0:T(512)S(1)}) all-reduce(f32[512]{0:T(512)S(1)} %get-tuple-element.18, f32[512]{0:T(512)S(1)} %get-tuple-element.13, f32[512]{0:T(512)S(1)} %get-tuple-element.12), channel_id=1, replica_groups=mesh['row'=16,'col'=2] {'row','col'}, use_global_device_ids=true, to_apply=%region_9.0 | all-reduce | flops 1536 | bytes 12288 | tf_op jit(solution)/shard_map/psum | solution.py:41
  203.7 0.6 fusion.3
  204.3 0.6 dynamic_slice.3
  (1 shorter events, 0.0 us)
Async XLA Ops:
  7.2 56.8 %all-gather.5.cloned.1.call-start = ((), (), s32[]{:S(2)}) async-start(), calls=%async_computation.1 | async-start | bytes 3899392 | tf_op jit(solution)/shard_map/all_gather | solution.py:31
  15.9 102.2 %all-gather.3.cloned.1.call-start = ((), (), s32[]{:S(2)}) async-start(), calls=%async_computation | async-start | bytes 5013504 | tf_op jit(solution)/shard_map/all_gather | solution.py:25
Sparse Core Ops, SparseCore 0:
  16.0 47.9 all-gather.4
  66.3 51.8 all-gather.2
where the time goes:
time: 214 us
  blocking collectives  94 us (44%)
  waiting for transfers between devices  90.8 us (42%)
  between operations  15.8 us (7%)
  matrix products  11.2 us (5%)
    all_gather x1, waiting for transfers between devices, per_device(): lax.all_gather(full_teacher, 'row', axis=0, tiled=True)  48.9 us
    all_gather x1, waiting for transfers between devices, per_device(): lax.all_gather(full_student, 'row', axis=0, tiled=True)  41.9 us
    psum x1, blocking collectives, per_device(): lax.psum((sum_teacher * teacher_scale, cross_term * teacher_scale, sum_st...  40 us
    pmax x1, blocking collectives, per_device(): lax.pmax((top_teacher, top_student), ('row', 'col'))  39.2 us
    all_gather x1, blocking collectives, per_device(): lax.all_gather(student_hidden, 'col', axis=1, tiled=True)  8.65 us
    all_gather x1, blocking collectives, per_device(): lax.all_gather(teacher_hidden, 'col', axis=1, tiled=True)  6.13 us
    dot_general x1, matrix products, per_device(): jnp.einsum('td,vd->tv', lax.all_gather(full_teacher, 'row', axis=0, tiled...  5.93 us
    dot_general x1, matrix products, per_device(): jnp.einsum('td,vd->tv', lax.all_gather(full_student, 'row', axis=0, tiled...  5.25 us
  transfers between devices with their start and end apart: 2, of which 2 were waited for; matrix products, arithmetic and copies ran while one was open for 2% of the time, Pallas kernels for 0%

commit v1 on v0

--- a/solution.py
+++ b/solution.py
@@ -2,6 +2,30 @@
 import jax.numpy as jnp
 from jax import lax
 from jax.sharding import PartitionSpec as P
+
+
+def work_both_ways(x, axis, dim, work, out_dim):
+    size, index, width = (lax.axis_size(axis), lax.axis_index(axis), x.shape[dim])
+    upward = [(i, (i + 1) % size) for i in range(size)]
+    left = [(b, a) for a, b in upward]
+    lower, upper = (lax.ppermute(x, axis, upward), lax.ppermute(x, axis, left))
+    made = work(x, index * width)
+    length = made.shape[out_dim]
+    out = jnp.zeros((*made.shape[:out_dim], size * length, *made.shape[out_dim + 1 :]), made.dtype)
+
+    def put(out, made, source):
+        return lax.dynamic_update_slice_in_dim(out, made, source * length, axis=out_dim)
+
+    out = put(out, made, index)
+    for lap in range(1, size // 2 + 1):
+        below, above = ((index - lap) % size, (index + lap) % size)
+        held = (lower, upper)
+        if lap < size // 2:
+            lower, upper = (lax.ppermute(lower, axis, upward), lax.ppermute(upper, axis, left))
+        out = put(out, work(held[0], below * width), below)
+        if 2 * lap < size:
+            out = put(out, work(held[1], above * width), above)
+    return out
 
 
 def block_stats(logit_teacher, logit_student):
@@ -26,11 +50,14 @@
         teacher_embed,
         preferred_element_type=jnp.float32,
     )
-    logit_student = jnp.einsum(
-        "td,vd->tv",
-        lax.all_gather(full_student, "row", axis=0, tiled=True),
-        student_embed,
-        preferred_element_type=jnp.float32,
+    logit_student = work_both_ways(
+        full_student,
+        "row",
+        0,
+        lambda part, offset: jnp.einsum(
+            "td,vd->tv", part, student_embed, preferred_element_type=jnp.float32
+        ),
+        0,
     )
     current = block_stats(logit_teacher, logit_student)
     partial_stats = tuple((fresh_rows for fresh_rows in current))

time: 214 us -> 240 us (1.12)
  waiting for transfers between devices: 90.8 us -> 7.94 us
  matrix products: 11.2 us -> 56.3 us
  local copies, waits for them, and re-layouts: 0.58 us -> 32.7 us
  starting transfers between devices: 0.08 us -> 32 us
    all_gather x1, waiting for transfers between devices: 48.9 us -> 0.01 us  [per_device(): lax.all_gather(full_teacher, 'row', axis=0, tiled=True)]
    dot_general x1 -> x16, matrix products: 5.25 us -> 50.4 us  [per_device(): jnp.einsum('td,vd->tv', part, student_embed, preferred_element_type=jnp.f...]
    all_gather x1 -> x0, waiting for transfers between devices: 41.9 us -> none  [per_device(): lax.all_gather(full_student, 'row', axis=0, tiled=True)]
    dynamic_update_slice x0 -> x16, local copies, waits for them, and re-layouts: none -> 32 us  [put(): lax.dynamic_update_slice_in_dim(out, made, source * length, axis=out_dim)]
    ppermute x0 -> x15, starting transfers between devices: none -> 31.9 us  [the longest x6 26.9 us: work_both_ways(): lax.ppermute(upper, axis, left)]
    ppermute x0 -> x15, waiting for transfers between devices: none -> 7.91 us  [the longest x6 5.21 us: work_both_ways(): lax.ppermute(upper, axis, left)]
    all_gather x1, blocking collectives: 6.13 us -> 9.37 us  [per_device(): lax.all_gather(teacher_hidden, 'col', axis=1, tiled=True)]
    all_gather x1, blocking collectives: 8.65 us -> 5.67 us  [per_device(): lax.all_gather(student_hidden, 'col', axis=1, tiled=True)]
  transfers between devices with their start and end apart: 2 -> 16, of which waited for: 2 -> 3; matrix products, arithmetic and copies ran while one was open for 2% -> 35% of each run, Pallas kernels for 0% -> 0%
where the time goes in v1:
time: 240 us; the launch traced here: 239 us
  blocking collectives  93 us (39%)
  matrix products  56.3 us (23%)
  local copies, waits for them, and re-layouts  32.7 us (14%)
  starting transfers between devices  32 us (13%)
  between operations  16.2 us (7%)
  waiting for transfers between devices  7.94 us (3%)
    dot_general x16, matrix products, per_device(): jnp.einsum('td,vd->tv', part, student_embed, preferred_element_type=jnp.f...  50.4 us
    psum x1, blocking collectives, per_device(): lax.psum((sum_teacher * teacher_scale, cross_term * teacher_scale, sum_st...  41.1 us
    pmax x1, blocking collectives, per_device(): lax.pmax((top_teacher, top_student), ('row', 'col'))  36.8 us
    dynamic_update_slice x16, local copies, waits for them, and re-layouts, put(): lax.dynamic_update_slice_in_dim(out, made, source * length, axis=out_dim)  32 us
    ppermute x6, starting transfers between devices, work_both_ways(): lax.ppermute(upper, axis, left)  26.9 us
    all_gather x1, blocking collectives, per_device(): lax.all_gather(teacher_hidden, 'col', axis=1, tiled=True)  9.37 us
    dot_general x1, matrix products, per_device(): jnp.einsum('td,vd->tv', lax.all_gather(full_teacher, 'row', axis=0, tiled...  5.95 us
    all_gather x1, blocking collectives, per_device(): lax.all_gather(student_hidden, 'col', axis=1, tiled=True)  5.67 us
  transfers between devices with their start and end apart: 16, of which 3 were waited for; matrix products, arithmetic and copies ran while one was open for 35% of the time, Pallas kernels for 0%

profile of v1, /device:TPU:0, one launch (start us, length us, event | category | flops | bytes accessed | tf_op | source)
XLA Modules:
  0.0 239.2 jit_solution(16968696900047661427)
XLA Ops:
  7.2 9.4 %all_gather.9 = bf16[32,4608]{1,0:T(8,128)(2,1)} all-gather(bf16[32,2304]{1,0:T(8,128)(2,1)} %param.4), channel_id=1, replica_groups=mesh['row'=16,'col'=2] {'col'}, dimensions={1}, use_global_device_ids=true | all-gather | bytes 442368 | tf_op jit(solution)/shard_map/all_gather | solution.py:44
  16.6 5.7 %all_gather.11 = bf16[32,3584]{1,0:T(8,128)(2,1)S(1)} all-gather(bf16[32,1792]{1,0:T(8,128)(2,1)} %param.5), channel_id=1, replica_groups=mesh['row'=16,'col'=2] {'col'}, dimensions={1}, use_global_device_ids=true | all-gather | bytes 344064 | tf_op jit(solution)/shard_map/all_gather | solution.py:45
  22.3 4.4 %collective-permute-start.1 = (bf16[32,3584]{1,0:T(8,128)(2,1)S(1)}, bf16[32,3584]{1,0:T(8,128)(2,1)S(1)}, u32[]{:S(2)}, u32[]{:S(2)}) collective-permute-start(bf16[32,3584]{1,0:T(8,128)(2,1)S(1)} %all_gather.11), channel_id=1, source_target_pairs={{2,0},{4,2},{6,4},{8,6},{10,8},{12,10},{14,12},{16,14},{18,16},{20... | collective-permute-start | bytes 688136 | tf_op jit(solution)/shard_map/ppermute | solution.py:11
  31.9 3.1 %fusion.6 = f32[32,512]{0,1:T(8,128)S(1)} fusion(bf16[32,3584]{1,0:T(8,128)(2,1)S(1)} %collective-permute-done, bf16[512,3584]{1,0:T(8,128)(2,1)} %param.7), kind=kOutput, calls=%fused_computation.12 | convolution fusion | flops 117440512 | bytes 3964928 | tf_op jit(solution)/shard_map/td,vd->tv/dot_general | solution.py:57
  36.6 3.1 %fusion.7 = f32[32,512]{0,1:T(8,128)S(1)} fusion(bf16[32,3584]{1,0:T(8,128)(2,1)S(1)} %collective-permute-done.1, bf16[512,3584]{1,0:T(8,128)(2,1)} %param.7), kind=kOutput, calls=%fused_computation.13 | convolution fusion | flops 117440512 | bytes 3964928 | tf_op jit(solution)/shard_map/td,vd->tv/dot_general | solution.py:57
  42.0 4.1 %collective-permute-start.3 = (bf16[32,3584]{1,0:T(8,128)(2,1)S(1)}, bf16[32,3584]{1,0:T(8,128)(2,1)S(1)}, u32[]{:S(2)}, u32[]{:S(2)}) collective-permute-start(bf16[32,3584]{1,0:T(8,128)(2,1)S(1)} %collective-permute-done.1), channel_id=1, source_target_pairs={{2,0},{4,2},{6,4},{8,6},{10,8},{12,10},{14,12},{16,14},{18,16},{20... | collective-permute-start | bytes 688136 | tf_op jit(solution)/shard_map/ppermute | solution.py:24
  46.1 3.7 %fusion.8 = f32[32,512]{0,1:T(8,128)S(1)} fusion(bf16[32,3584]{1,0:T(8,128)(2,1)S(1)} %collective-permute-done.2, bf16[512,3584]{1,0:T(8,128)(2,1)} %param.7), kind=kOutput, calls=%fused_computation.14 | convolution fusion | flops 117440512 | bytes 3964928 | tf_op jit(solution)/shard_map/td,vd->tv/dot_general | solution.py:57
  54.3 3.1 %fusion.9 = f32[32,512]{0,1:T(8,128)S(1)} fusion(bf16[32,3584]{1,0:T(8,128)(2,1)S(1)} %collective-permute-done.3, bf16[512,3584]{1,0:T(8,128)(2,1)} %param.7), kind=kOutput, calls=%fused_computation.15 | convolution fusion | flops 117440512 | bytes 3964928 | tf_op jit(solution)/shard_map/td,vd->tv/dot_general | solution.py:57
  59.7 4.7 %collective-permute-start.5 = (bf16[32,3584]{1,0:T(8,128)(2,1)S(1)}, bf16[32,3584]{1,0:T(8,128)(2,1)S(1)}, u32[]{:S(2)}, u32[]{:S(2)}) collective-permute-start(bf16[32,3584]{1,0:T(8,128)(2,1)S(1)} %collective-permute-done.3), channel_id=1, source_target_pairs={{2,0},{4,2},{6,4},{8,6},{10,8},{12,10},{14,12},{16,14},{18,16},{20... | collective-permute-start | bytes 688136 | tf_op jit(solution)/shard_map/ppermute | solution.py:24
  64.4 3.1 %fusion.10 = f32[32,512]{0,1:T(8,128)S(1)} fusion(bf16[32,3584]{1,0:T(8,128)(2,1)S(1)} %collective-permute-done.4, bf16[512,3584]{1,0:T(8,128)(2,1)} %param.7), kind=kOutput, calls=%fused_computation.16 | convolution fusion | flops 117440512 | bytes 3964928 | tf_op jit(solution)/shard_map/td,vd->tv/dot_general | solution.py:57
  71.3 3.1 %fusion.11 = f32[32,512]{0,1:T(8,128)S(1)} fusion(bf16[32,3584]{1,0:T(8,128)(2,1)S(1)} %collective-permute-done.5, bf16[512,3584]{1,0:T(8,128)(2,1)} %param.7), kind=kOutput, calls=%fused_computation.17 | convolution fusion | flops 117440512 | bytes 3964928 | tf_op jit(solution)/shard_map/td,vd->tv/dot_general | solution.py:57
  76.7 4.7 %collective-permute-start.7 = (bf16[32,3584]{1,0:T(8,128)(2,1)S(1)}, bf16[32,3584]{1,0:T(8,128)(2,1)S(1)}, u32[]{:S(2)}, u32[]{:S(2)}) collective-permute-start(bf16[32,3584]{1,0:T(8,128)(2,1)S(1)} %collective-permute-done.5), channel_id=1, source_target_pairs={{2,0},{4,2},{6,4},{8,6},{10,8},{12,10},{14,12},{16,14},{18,16},{20... | collective-permute-start | bytes 688136 | tf_op jit(solution)/shard_map/ppermute | solution.py:24
  90.7 4.9 %collective-permute-start.9 = (bf16[32,3584]{1,0:T(8,128)(2,1)S(1)}, bf16[32,3584]{1,0:T(8,128)(2,1)S(1)}, u32[]{:S(2)}, u32[]{:S(2)}) collective-permute-start(bf16[32,3584]{1,0:T(8,128)(2,1)S(1)} %collective-permute-done.7), channel_id=1, source_target_pairs={{2,0},{4,2},{6,4},{8,6},{10,8},{12,10},{14,12},{16,14},{18,16},{20... | collective-permute-start | bytes 688136 | tf_op jit(solution)/shard_map/ppermute | solution.py:24
  95.6 3.1 %fusion.14 = f32[32,512]{0,1:T(8,128)S(1)} fusion(bf16[32,3584]{1,0:T(8,128)(2,1)S(1)} %collective-permute-done.8, bf16[512,3584]{1,0:T(8,128)(2,1)} %param.7), kind=kOutput, calls=%fused_computation.20 | convolution fusion | flops 117440512 | bytes 3964928 | tf_op jit(solution)/shard_map/td,vd->tv/dot_general | solution.py:57
  101.3 3.1 %fusion.15 = f32[32,512]{0,1:T(8,128)S(1)} fusion(bf16[32,3584]{1,0:T(8,128)(2,1)S(1)} %collective-permute-done.9, bf16[512,3584]{1,0:T(8,128)(2,1)} %param.7), kind=kOutput, calls=%fused_computation.21 | convolution fusion | flops 117440512 | bytes 3964928 | tf_op jit(solution)/shard_map/td,vd->tv/dot_general | solution.py:57
  106.7 4.1 %collective-permute-start.11 = (bf16[32,3584]{1,0:T(8,128)(2,1)S(1)}, bf16[32,3584]{1,0:T(8,128)(2,1)S(1)}, u32[]{:S(2)}, u32[]{:S(2)}) collective-permute-start(bf16[32,3584]{1,0:T(8,128)(2,1)S(1)} %collective-permute-done.9), channel_id=1, source_target_pairs={{2,0},{4,2},{6,4},{8,6},{10,8},{12,10},{14,12},{16,14},{18,16},{20... | collective-permute-start | bytes 688136 | tf_op jit(solution)/shard_map/ppermute | solution.py:24
  110.8 3.1 %fusion.16 = f32[32,512]{0,1:T(8,128)S(1)} fusion(bf16[32,3584]{1,0:T(8,128)(2,1)S(1)} %collective-permute-done.10, bf16[512,3584]{1,0:T(8,128)(2,1)} %param.7), kind=kOutput, calls=%fused_computation.22 | convolution fusion | flops 117440512 | bytes 3964928 | tf_op jit(solution)/shard_map/td,vd->tv/dot_general | solution.py:57
  116.3 3.1 %fusion.17 = f32[32,512]{0,1:T(8,128)S(1)} fusion(bf16[32,3584]{1,0:T(8,128)(2,1)S(1)} %collective-permute-done.11, bf16[512,3584]{1,0:T(8,128)(2,1)} %param.7), kind=kOutput, calls=%fused_computation.23 | convolution fusion | flops 117440512 | bytes 3964928 | tf_op jit(solution)/shard_map/td,vd->tv/dot_general | solution.py:57
  121.8 4.5 %collective-permute-start.13 = (bf16[32,3584]{1,0:T(8,128)(2,1)S(1)}, bf16[32,3584]{1,0:T(8,128)(2,1)S(1)}, u32[]{:S(2)}, u32[]{:S(2)}) collective-permute-start(bf16[32,3584]{1,0:T(8,128)(2,1)S(1)} %collective-permute-done.11), channel_id=1, source_target_pairs={{2,0},{4,2},{6,4},{8,6},{10,8},{12,10},{14,12},{16,14},{18,16},{20... | collective-permute-start | bytes 688136 | tf_op jit(solution)/shard_map/ppermute | solution.py:24
  126.2 3.1 %fusion.18 = f32[32,512]{0,1:T(8,128)S(1)} fusion(bf16[32,3584]{1,0:T(8,128)(2,1)S(1)} %collective-permute-done.12, bf16[512,3584]{1,0:T(8,128)(2,1)} %param.7), kind=kOutput, calls=%fused_computation.24 | convolution fusion | flops 117440512 | bytes 3964928 | tf_op jit(solution)/shard_map/td,vd->tv/dot_general | solution.py:57
  131.8 3.1 %fusion.19 = f32[32,512]{0,1:T(8,128)S(1)} fusion(bf16[32,3584]{1,0:T(8,128)(2,1)S(1)} %collective-permute-done.13, bf16[512,3584]{1,0:T(8,128)(2,1)} %param.7), kind=kOutput, calls=%fused_computation.25 | convolution fusion | flops 117440512 | bytes 3964928 | tf_op jit(solution)/shard_map/td,vd->tv/dot_general | solution.py:57
  145.0 5.9 %fusion.4 = (f32[512]{0:T(512)S(1)}, f32[512,512]{0,1:T(8,128)S(1)}) fusion(bf16[512,4608]{1,0:T(8,128)(2,1)} %all-gather.2.cloned.1.call-done, bf16[512,4608]{1,0:T(8,128)(2,1)} %param.6), kind=kOutput, calls=%fused_computation.10 | convolution fusion | flops 2416180736 | bytes 10487808 | tf_op jit(solution)/shard_map/td,vd->tv/dot_general | solution.py:47
  151.0 36.8 %all-reduce.1 = (f32[512]{0:T(512)S(1)}, f32[512]{0:T(512)S(1)}) all-reduce(f32[512]{0:T(512)S(1)} %reduce_max.19, f32[512]{0:T(512)S(1)} %get-tuple-element.14), channel_id=1, replica_groups=mesh['row'=16,'col'=2] {'row','col'}, use_global_device_ids=true, to_apply=%region_7.8 | all-reduce | flops 1024 | bytes 8192 | tf_op jit(solution)/shard_map/pmax | solution.py:65
  188.3 41.1 %all-reduce = (f32[512]{0:T(512)S(1)}, f32[512]{0:T(512)S(1)}, f32[512]{0:T(512)S(1)}) all-reduce(f32[512]{0:T(512)S(1)} %get-tuple-element.16, f32[512]{0:T(512)S(1)} %get-tuple-element.13, f32[512]{0:T(512)S(1)} %get-tuple-element.12), channel_id=1, replica_groups=mesh['row'=16,'col'=2] {'row','col'}, use_global_device_ids=true, to_apply=%region_9.10 | all-reduce | flops 1536 | bytes 12288 | tf_op jit(solution)/shard_map/psum | solution.py:68
  (52 shorter events, 54.8 us)
Async XLA Ops:
  7.2 137.9 %all-gather.2.cloned.1.call-start = ((), (), s32[]{:S(2)}) async-start(), calls=%async_computation | async-start | bytes 5013504 | tf_op jit(solution)/shard_map/all_gather | solution.py:49
  22.3 9.6 %collective-permute-start = (bf16[32,3584]{1,0:T(8,128)(2,1)S(1)}, bf16[32,3584]{1,0:T(8,128)(2,1)S(1)}, u32[]{:S(2)}, u32[]{:S(2)}) collective-permute-start(bf16[32,3584]{1,0:T(8,128)(2,1)S(1)} %all_gather.11), channel_id=1, source_target_pairs={{0,2},{2,4},{4,6},{6,8},{8,10},{10,12},{12,14},{14,16},{16,18},{18... | collective-permute-start | bytes 688136 | tf_op jit(solution)/shard_map/ppermute | solution.py:11
  22.3 14.3 %collective-permute-start.1 = (bf16[32,3584]{1,0:T(8,128)(2,1)S(1)}, bf16[32,3584]{1,0:T(8,128)(2,1)S(1)}, u32[]{:S(2)}, u32[]{:S(2)}) collective-permute-start(bf16[32,3584]{1,0:T(8,128)(2,1)S(1)} %all_gather.11), channel_id=1, source_target_pairs={{2,0},{4,2},{6,4},{8,6},{10,8},{12,10},{14,12},{16,14},{18,16},{20... | collective-permute-start | bytes 688136 | tf_op jit(solution)/shard_map/ppermute | solution.py:11
  36.5 9.6 %collective-permute-start.2 = (bf16[32,3584]{1,0:T(8,128)(2,1)S(1)}, bf16[32,3584]{1,0:T(8,128)(2,1)S(1)}, u32[]{:S(2)}, u32[]{:S(2)}) collective-permute-start(bf16[32,3584]{1,0:T(8,128)(2,1)S(1)} %collective-permute-done), channel_id=1, source_target_pairs={{0,2},{2,4},{4,6},{6,8},{8,10},{10,12},{12,14},{14,16},{16,18},{18... | collective-permute-start | bytes 688136 | tf_op jit(solution)/shard_map/ppermute | solution.py:24
  42.0 12.3 %collective-permute-start.3 = (bf16[32,3584]{1,0:T(8,128)(2,1)S(1)}, bf16[32,3584]{1,0:T(8,128)(2,1)S(1)}, u32[]{:S(2)}, u32[]{:S(2)}) collective-permute-start(bf16[32,3584]{1,0:T(8,128)(2,1)S(1)} %collective-permute-done.1), channel_id=1, source_target_pairs={{2,0},{4,2},{6,4},{8,6},{10,8},{12,10},{14,12},{16,14},{18,16},{20... | collective-permute-start | bytes 688136 | tf_op jit(solution)/shard_map/ppermute | solution.py:24
  51.2 13.2 %collective-permute-start.4 = (bf16[32,3584]{1,0:T(8,128)(2,1)S(1)}, bf16[32,3584]{1,0:T(8,128)(2,1)S(1)}, u32[]{:S(2)}, u32[]{:S(2)}) collective-permute-start(bf16[32,3584]{1,0:T(8,128)(2,1)S(1)} %collective-permute-done.2), channel_id=1, source_target_pairs={{0,2},{2,4},{4,6},{6,8},{8,10},{10,12},{12,14},{14,16},{16,18},{18... | collective-permute-start | bytes 688136 | tf_op jit(solution)/shard_map/ppermute | solution.py:24
  59.7 11.5 %collective-permute-start.5 = (bf16[32,3584]{1,0:T(8,128)(2,1)S(1)}, bf16[32,3584]{1,0:T(8,128)(2,1)S(1)}, u32[]{:S(2)}, u32[]{:S(2)}) collective-permute-start(bf16[32,3584]{1,0:T(8,128)(2,1)S(1)} %collective-permute-done.3), channel_id=1, source_target_pairs={{2,0},{4,2},{6,4},{8,6},{10,8},{12,10},{14,12},{16,14},{18,16},{20... | collective-permute-start | bytes 688136 | tf_op jit(solution)/shard_map/ppermute | solution.py:24
  69.0 12.4 %collective-permute-start.6 = (bf16[32,3584]{1,0:T(8,128)(2,1)S(1)}, bf16[32,3584]{1,0:T(8,128)(2,1)S(1)}, u32[]{:S(2)}, u32[]{:S(2)}) collective-permute-start(bf16[32,3584]{1,0:T(8,128)(2,1)S(1)} %collective-permute-done.4), channel_id=1, source_target_pairs={{0,2},{2,4},{4,6},{6,8},{8,10},{10,12},{12,14},{14,16},{16,18},{18... | collective-permute-start | bytes 688136 | tf_op jit(solution)/shard_map/ppermute | solution.py:24
  76.7 9.0 %collective-permute-start.7 = (bf16[32,3584]{1,0:T(8,128)(2,1)S(1)}, bf16[32,3584]{1,0:T(8,128)(2,1)S(1)}, u32[]{:S(2)}, u32[]{:S(2)}) collective-permute-start(bf16[32,3584]{1,0:T(8,128)(2,1)S(1)} %collective-permute-done.5), channel_id=1, source_target_pairs={{2,0},{4,2},{6,4},{8,6},{10,8},{12,10},{14,12},{16,14},{18,16},{20... | collective-permute-start | bytes 688136 | tf_op jit(solution)/shard_map/ppermute | solution.py:24
  85.6 10.0 %collective-permute-start.8 = (bf16[32,3584]{1,0:T(8,128)(2,1)S(1)}, bf16[32,3584]{1,0:T(8,128)(2,1)S(1)}, u32[]{:S(2)}, u32[]{:S(2)}) collective-permute-start(bf16[32,3584]{1,0:T(8,128)(2,1)S(1)} %collective-permute-done.6), channel_id=1, source_target_pairs={{0,2},{2,4},{4,6},{6,8},{8,10},{10,12},{12,14},{14,16},{16,18},{18... | collective-permute-start | bytes 688136 | tf_op jit(solution)/shard_map/ppermute | solution.py:24
  90.7 10.5 %collective-permute-start.9 = (bf16[32,3584]{1,0:T(8,128)(2,1)S(1)}, bf16[32,3584]{1,0:T(8,128)(2,1)S(1)}, u32[]{:S(2)}, u32[]{:S(2)}) collective-permute-start(bf16[32,3584]{1,0:T(8,128)(2,1)S(1)} %collective-permute-done.7), channel_id=1, source_target_pairs={{2,0},{4,2},{6,4},{8,6},{10,8},{12,10},{14,12},{16,14},{18,16},{20... | collective-permute-start | bytes 688136 | tf_op jit(solution)/shard_map/ppermute | solution.py:24
  101.0 9.8 %collective-permute-start.10 = (bf16[32,3584]{1,0:T(8,128)(2,1)S(1)}, bf16[32,3584]{1,0:T(8,128)(2,1)S(1)}, u32[]{:S(2)}, u32[]{:S(2)}) collective-permute-start(bf16[32,3584]{1,0:T(8,128)(2,1)S(1)} %collective-permute-done.8), channel_id=1, source_target_pairs={{0,2},{2,4},{4,6},{6,8},{8,10},{10,12},{12,14},{14,16},{16,18},{18... | collective-permute-start | bytes 688136 | tf_op jit(solution)/shard_map/ppermute | solution.py:24
  106.7 9.6 %collective-permute-start.11 = (bf16[32,3584]{1,0:T(8,128)(2,1)S(1)}, bf16[32,3584]{1,0:T(8,128)(2,1)S(1)}, u32[]{:S(2)}, u32[]{:S(2)}) collective-permute-start(bf16[32,3584]{1,0:T(8,128)(2,1)S(1)} %collective-permute-done.9), channel_id=1, source_target_pairs={{2,0},{4,2},{6,4},{8,6},{10,8},{12,10},{14,12},{16,14},{18,16},{20... | collective-permute-start | bytes 688136 | tf_op jit(solution)/shard_map/ppermute | solution.py:24
  116.2 10.0 %collective-permute-start.12 = (bf16[32,3584]{1,0:T(8,128)(2,1)S(1)}, bf16[32,3584]{1,0:T(8,128)(2,1)S(1)}, u32[]{:S(2)}, u32[]{:S(2)}) collective-permute-start(bf16[32,3584]{1,0:T(8,128)(2,1)S(1)} %collective-permute-done.10), channel_id=1, source_target_pairs={{0,2},{2,4},{4,6},{6,8},{8,10},{10,12},{12,14},{14,16},{16,18},{18... | collective-permute-start | bytes 688136 | tf_op jit(solution)/shard_map/ppermute | solution.py:24
  121.8 10.0 %collective-permute-start.13 = (bf16[32,3584]{1,0:T(8,128)(2,1)S(1)}, bf16[32,3584]{1,0:T(8,128)(2,1)S(1)}, u32[]{:S(2)}, u32[]{:S(2)}) collective-permute-start(bf16[32,3584]{1,0:T(8,128)(2,1)S(1)} %collective-permute-done.11), channel_id=1, source_target_pairs={{2,0},{4,2},{6,4},{8,6},{10,8},{12,10},{14,12},{16,14},{18,16},{20... | collective-permute-start | bytes 688136 | tf_op jit(solution)/shard_map/ppermute | solution.py:24
  131.7 8.2 %collective-permute-start.14 = (bf16[32,3584]{1,0:T(8,128)(2,1)S(1)}, bf16[32,3584]{1,0:T(8,128)(2,1)S(1)}, u32[]{:S(2)}, u32[]{:S(2)}) collective-permute-start(bf16[32,3584]{1,0:T(8,128)(2,1)S(1)} %collective-permute-done.12), channel_id=1, source_target_pairs={{0,2},{2,4},{4,6},{6,8},{8,10},{10,12},{12,14},{14,16},{16,18},{18... | collective-permute-start | bytes 688136 | tf_op jit(solution)/shard_map/ppermute | solution.py:24
Sparse Core Ops, SparseCore 0:
  16.7 62.1 all-gather.1
